TPU v7x, 32 devices: a whole 2x2x4 slice. The times are simulated.
32 devices in a mesh: dp: 8 (over z, x), tensor: 4 (over y, core).
Axes of the slice: x: 2, y: 2, z: 4, core: 2. Of those that a mesh axis runs over, the one named last changes fastest.
Arguments:
- tokens: bfloat16 [32768, 1024], P('dp', 'tensor'), may hold values from -6 to 6
- lengths: int32 [16], P('dp'), may hold values from 512 to 2048, as said below
- grad_out: bfloat16 [32768, 1024], P('dp', 'tensor'), may hold values from -6 to 6
- norm_gain: bfloat16 [1024], P('dp'), may hold values from 0.099609375 to 1.8984375
- w_gate: bfloat16 [1024, 2048], P('dp', 'tensor'), may hold values from -0.1875 to 0.1875
- w_value: bfloat16 [1024, 2048], P('dp', 'tensor'), may hold values from -0.1875 to 0.1875
- w_bc: bfloat16 [1024, 256], P('dp'), may hold values from -0.1875 to 0.1875
- w_dt: bfloat16 [1024, 32], P('dp', 'tensor'), may hold values from -0.1875 to 0.1875
- conv_x: float32 [5, 2048], P(None, 'tensor'), may hold values from -3 to 3
- conv_bc: float32 [5, 256], replicated, may hold values from -3 to 3
- dt_bias: float32 [32], P('tensor'), may hold values from -7 to -2.5
- a_log: float32 [32], P('tensor'), may hold values from 0 to 2.77
- skip_d: float32 [32], P('tensor'), may hold values from 0.35 to 2.75
- gate_gain: float32 [2048], P('tensor'), may hold values from 0.1 to 1.9
- w_out: bfloat16 [1024, 2048], P('dp', 'tensor'), may hold values from -0.125 to 0.125
Outputs:
- out: bfloat16 [32768, 1024], P('dp', 'tensor')
- grad_tokens: float32 [32768, 1024], P('dp', 'tensor')
- grad_norm_gain: float32 [1024], P(('dp', 'tensor'))
- grad_w_gate: float32 [1024, 2048], P('dp', 'tensor')
- grad_w_value: float32 [1024, 2048], P('dp', 'tensor')
- grad_w_bc: float32 [1024, 256], P(('dp', 'tensor'))
- grad_w_dt: float32 [1024, 32], P('dp', 'tensor')
- grad_conv_x: float32 [5, 2048], P(None, 'tensor')
- grad_conv_bc: float32 [5, 256], replicated
- grad_dt_bias: float32 [32], P('tensor')
- grad_a_log: float32 [32], P('tensor')
- grad_skip_d: float32 [32], P('tensor')
- grad_gate_gain: float32 [2048], P('tensor')
- grad_w_out: float32 [1024, 2048], P('dp', 'tensor')
Inputs may be any that keep to these rules, and one draw needn't show every extreme that they name: Sequence i occupies the first lengths[i] of its 2048 slots; the rest is padding. Sequence 0 is full.
All inputs are finite; a program needn't handle non-finite values.
Results may differ from a plain program's by a relative error of at most 0.0085.
Values may be sent and summed in bfloat16 or wider, within the bound.
No kernel may reach another device: no remote copies, remote signals or barrier semaphores. Data moves between devices by JAX's collectives and lax.ppermute only.
A program may use at most 192 MiB of HBM per device.

v0:
```python
import jax
import jax.numpy as jnp
from jax import lax
from jax.sharding import PartitionSpec as P

GROUP = 256
SEQ_LEN = 2048
epsilon = 1e-05


def causal_conv(signal, kernel):
    window = kernel.shape[0] - 1
    length = signal.shape[0]
    padded = jnp.concatenate([jnp.zeros((window - 1, signal.shape[1]), jnp.float32), signal], 0)
    summed = jnp.broadcast_to(kernel[window], signal.shape)
    for offset in range(window):
        summed = summed + kernel[offset] * padded[offset : offset + length]
    return summed


def group_scan(values, step_sizes, decay_rates, inputs_b, inputs_c):
    length, head_count, head_width = values.shape
    blocks = length // GROUP
    values = values.reshape(blocks, GROUP, head_count, head_width)
    step_sizes = step_sizes.reshape(blocks, GROUP, head_count)
    inputs_b = inputs_b.reshape(blocks, GROUP, -1)
    inputs_c = inputs_c.reshape(blocks, GROUP, -1)
    log_decay = jnp.transpose(step_sizes * decay_rates, (0, 2, 1))
    running = jnp.cumsum(log_decay, axis=2)
    causal = jnp.arange(GROUP)[:, None] >= jnp.arange(GROUP)[None, :]
    decay_grid = jnp.exp(jnp.where(causal, running[..., :, None] - running[..., None, :], -jnp.inf))
    intersection = jnp.einsum("bqn,bsn->bqs", inputs_c, inputs_b, precision=lax.Precision.HIGHEST)
    weighted = values * step_sizes[..., None]
    inner_part = jnp.einsum(
        "bhqs,bshp->bqhp",
        intersection[:, None] * decay_grid,
        weighted,
        precision=lax.Precision.HIGHEST,
    )
    to_end = jnp.exp(running[..., -1:] - running)
    states = jnp.einsum(
        "bsn,bhs,bshp->bhpn", inputs_b, to_end, weighted, precision=lax.Precision.HIGHEST
    )
    totals = running[..., -1]
    through = jnp.cumsum(totals, axis=0)
    before = through - totals
    earlier = jnp.arange(blocks)[:, None] > jnp.arange(blocks)[None, :]
    carry_weights = jnp.exp(
        jnp.where(earlier[..., None], before[:, None, :] - through[None, :, :], -jnp.inf)
    )
    incoming = jnp.einsum("cdh,dhpn->chpn", carry_weights, states, precision=lax.Precision.HIGHEST)
    outer_part = jnp.einsum(
        "bqn,bhpn,bhq->bqhp", inputs_c, incoming, jnp.exp(running), precision=lax.Precision.HIGHEST
    )
    return (inner_part + outer_part).reshape(length, head_count, head_width)


def mixer(
    gate_in, value_in, shared_in, step_in, conv_value, conv_shared, step_bias, log_rate, skip_gain
):
    length = value_in.shape[0]
    head_count = step_in.shape[1]
    state_size = shared_in.shape[1] // 2
    convolved = jax.nn.silu(causal_conv(value_in, conv_value))
    shared = jax.nn.silu(causal_conv(shared_in, conv_shared))
    step_sizes = jax.nn.softplus(step_in + step_bias)
    decay_rates = -jnp.exp(log_rate)
    values = convolved.reshape(length, head_count, -1)
    scanned = group_scan(
        values, step_sizes, decay_rates, shared[:, :state_size], shared[:, state_size:]
    )
    mixed_out = scanned + skip_gain[:, None] * values
    return mixed_out.reshape(length, -1) * jax.nn.silu(gate_in)


def over_rows(left, right):
    return lax.dot_general(
        left, right, (((0,), (0,)), ((), ())), preferred_element_type=jnp.float32
    )


def against(left, right):
    return lax.dot_general(
        left, right, (((1,), (1,)), ((), ())), preferred_element_type=jnp.float32
    )


def per_device(
    tokens,
    lengths,
    grad_out,
    norm_gain,
    w_gate,
    w_value,
    w_bc,
    w_dt,
    conv_x,
    conv_bc,
    dt_bias,
    a_log,
    skip_d,
    gate_gain,
    w_out,
):
    tensor_count = lax.axis_size("tensor")
    row_count, local_width = tokens.shape
    width_all = local_width * tensor_count
    inner_local = w_gate.shape[1]
    inner_all = inner_local * tensor_count
    micro_count = row_count // SEQ_LEN

    def micro_step(micro_index, carry):
        (
            out_rows,
            grad_rows,
            acc_gate,
            acc_value,
            acc_shared,
            acc_step,
            acc_out,
            acc_norm,
            acc_conv_value,
            acc_conv_shared,
            acc_bias,
            acc_rate,
            acc_skip,
            acc_gain,
        ) = carry
        start = micro_index * SEQ_LEN
        local_rows = lax.dynamic_slice_in_dim(tokens, start, SEQ_LEN, 0)
        local_cot = lax.dynamic_slice_in_dim(grad_out, start, SEQ_LEN, 0)
        seq_length = lax.dynamic_slice_in_dim(lengths, micro_index, 1, 0)[0]
        valid = (jnp.arange(SEQ_LEN) < seq_length)[:, None]
        forward_weights = (
            lax.all_gather(norm_gain, "dp", axis=0, tiled=True),
            lax.all_gather(w_gate, "dp", axis=0, tiled=True),
            lax.all_gather(w_value, "dp", axis=0, tiled=True),
            lax.all_gather(w_bc, "dp", axis=0, tiled=True),
            lax.all_gather(w_dt, "dp", axis=0, tiled=True),
            lax.all_gather(w_out, "dp", axis=0, tiled=True),
        )
        gain_rows, gate_rows, value_rows, shared_rows, step_rows, out_weight = forward_weights
        full_rows = lax.all_gather(local_rows, "tensor", axis=1, tiled=True)
        xfloat = full_rows.astype(jnp.float32)
        inverse_rms = lax.rsqrt(jnp.mean(xfloat * xfloat, -1, keepdims=True) + epsilon)
        gain_float = gain_rows.astype(jnp.float32)
        normed = (xfloat * inverse_rms * gain_float).astype(jnp.bfloat16)
        gate_proj = jnp.dot(normed, gate_rows, preferred_element_type=jnp.float32)
        value_proj = jnp.dot(normed, value_rows, preferred_element_type=jnp.float32)
        shared_in = jnp.dot(normed, shared_rows, preferred_element_type=jnp.float32)
        step_in = jnp.dot(normed, step_rows, preferred_element_type=jnp.float32)
        mixed_out, mixer_back = jax.vjp(
            mixer,
            gate_proj,
            value_proj,
            shared_in,
            step_in,
            conv_x,
            conv_bc,
            dt_bias,
            a_log,
            skip_d,
        )
        squares = lax.psum(jnp.sum(mixed_out * mixed_out, -1), "tensor")
        inverse_gate = lax.rsqrt(squares / inner_all + epsilon)[:, None]
        normed_out = (mixed_out * inverse_gate * gate_gain).astype(jnp.bfloat16)
        row_block = lax.all_to_all(normed_out, "tensor", split_axis=0, concat_axis=1, tiled=True)
        out_full = lax.all_gather(out_weight, "tensor", axis=1, tiled=True)
        branch_rows = lax.all_to_all(
            against(row_block, out_full).astype(jnp.bfloat16),
            "tensor",
            split_axis=1,
            concat_axis=0,
            tiled=True,
        ).astype(jnp.float32)
        out_local = (local_rows.astype(jnp.float32) + jnp.where(valid, branch_rows, 0.0)).astype(
            jnp.bfloat16
        )
        cotangent = jnp.where(valid, local_cot, jnp.zeros_like(local_cot))
        full_cot = lax.all_gather(cotangent, "tensor", axis=1, tiled=True)
        backward_weights = (
            lax.all_gather(norm_gain, "dp", axis=0, tiled=True),
            lax.all_gather(w_gate, "dp", axis=0, tiled=True),
            lax.all_gather(w_value, "dp", axis=0, tiled=True),
            lax.all_gather(w_bc, "dp", axis=0, tiled=True),
            lax.all_gather(w_dt, "dp", axis=0, tiled=True),
            lax.all_gather(w_out, "dp", axis=0, tiled=True),
        )
        gain_back, gate_back, value_back, shared_back, step_back, out_back = backward_weights
        acc_out = acc_out + over_rows(full_cot, normed_out)
        grad_normed_out = jnp.dot(full_cot, out_back, preferred_element_type=jnp.float32)
        acc_gain = acc_gain + jnp.sum(grad_normed_out * mixed_out * inverse_gate, 0)
        inner_sum = lax.psum(jnp.sum(grad_normed_out * gate_gain * mixed_out, -1), "tensor")
        grad_mixed = (
            inverse_gate * gate_gain * grad_normed_out
            - mixed_out * inverse_gate**3 * inner_sum[:, None] / inner_all
        )
        (
            grad_gate,
            grad_value,
            grad_shared,
            grad_step,
            grad_conv_value,
            grad_conv_shared,
            grad_bias,
            grad_rate,
            grad_skip,
        ) = mixer_back(grad_mixed)
        gate_low = grad_gate.astype(jnp.bfloat16)
        value_low = grad_value.astype(jnp.bfloat16)
        shared_low = grad_shared.astype(jnp.bfloat16)
        step_low = grad_step.astype(jnp.bfloat16)
        grad_normed = (
            against(gate_low, gate_back)
            + against(value_low, value_back)
            + against(shared_low, shared_back)
            + against(step_low, step_back)
        )
        acc_gate = acc_gate + over_rows(normed, gate_low)
        acc_value = acc_value + over_rows(normed, value_low)
        acc_shared = acc_shared + over_rows(normed, shared_low)
        acc_step = acc_step + over_rows(normed, step_low)
        gain_back_float = gain_back.astype(jnp.float32)
        acc_norm = acc_norm + jnp.sum(grad_normed * xfloat * inverse_rms, 0)
        grad_input = (
            inverse_rms * gain_back_float * grad_normed
            - xfloat
            * inverse_rms**3
            * jnp.sum(grad_normed * gain_back_float * xfloat, -1, keepdims=True)
            / width_all
        )
        grad_local = lax.psum_scatter(
            grad_input.astype(jnp.bfloat16), "tensor", scatter_dimension=1, tiled=True
        ).astype(jnp.float32) + cotangent.astype(jnp.float32)
        out_rows = lax.dynamic_update_slice_in_dim(out_rows, out_local, start, 0)
        grad_rows = lax.dynamic_update_slice_in_dim(grad_rows, grad_local, start, 0)
        return (
            out_rows,
            grad_rows,
            acc_gate,
            acc_value,
            acc_shared,
            acc_step,
            acc_out,
            acc_norm,
            acc_conv_value + grad_conv_value,
            acc_conv_shared + grad_conv_shared,
            acc_bias + grad_bias,
            acc_rate + grad_rate,
            acc_skip + grad_skip,
            acc_gain,
        )

    initial = (
        jnp.zeros((row_count, local_width), jnp.bfloat16),
        jnp.zeros((row_count, local_width), jnp.float32),
        jnp.zeros((width_all, inner_local), jnp.float32),
        jnp.zeros((width_all, inner_local), jnp.float32),
        jnp.zeros((width_all, w_bc.shape[1]), jnp.float32),
        jnp.zeros((width_all, w_dt.shape[1]), jnp.float32),
        jnp.zeros((width_all, inner_local), jnp.float32),
        jnp.zeros((width_all,), jnp.float32),
        jnp.zeros_like(conv_x),
        jnp.zeros_like(conv_bc),
        jnp.zeros_like(dt_bias),
        jnp.zeros_like(a_log),
        jnp.zeros_like(skip_d),
        jnp.zeros_like(gate_gain),
    )
    final = lax.fori_loop(0, micro_count, micro_step, initial)
    (
        out_rows,
        grad_rows,
        acc_gate,
        acc_value,
        acc_shared,
        acc_step,
        acc_out,
        acc_norm,
        acc_conv_value,
        acc_conv_shared,
        acc_bias,
        acc_rate,
        acc_skip,
        acc_gain,
    ) = final
    grad_gate_rows, grad_value_rows, grad_step_rows, grad_out_rows = (
        lax.psum_scatter(acc_gate, "dp", scatter_dimension=0, tiled=True),
        lax.psum_scatter(acc_value, "dp", scatter_dimension=0, tiled=True),
        lax.psum_scatter(acc_step, "dp", scatter_dimension=0, tiled=True),
        lax.psum_scatter(acc_out, "dp", scatter_dimension=0, tiled=True),
    )
    grad_shared_rows, grad_norm_rows = (
        lax.psum_scatter(acc_shared, ("dp", "tensor"), scatter_dimension=0, tiled=True),
        lax.psum_scatter(acc_norm, ("dp", "tensor"), scatter_dimension=0, tiled=True),
    )
    grad_conv_value, grad_bias, grad_rate, grad_skip, grad_gain = lax.psum(
        (acc_conv_value, acc_bias, acc_rate, acc_skip, acc_gain), "dp"
    )
    grad_conv_shared = lax.psum(acc_conv_shared, ("dp", "tensor"))
    return (
        out_rows,
        grad_rows,
        grad_norm_rows,
        grad_gate_rows,
        grad_value_rows,
        grad_shared_rows,
        grad_step_rows,
        grad_conv_value,
        grad_conv_shared,
        grad_bias,
        grad_rate,
        grad_skip,
        grad_gain,
        grad_out_rows,
    )


def solution(mesh):
    return jax.shard_map(
        per_device,
        mesh=mesh,
        in_specs=(
            P("dp", "tensor"),
            P("dp"),
            P("dp", "tensor"),
            P("dp"),
            P("dp", "tensor"),
            P("dp", "tensor"),
            P("dp", None),
            P("dp", "tensor"),
            P(None, "tensor"),
            P(),
            P("tensor"),
            P("tensor"),
            P("tensor"),
            P("tensor"),
            P("dp", "tensor"),
        ),
        out_specs=(
            P("dp", "tensor"),
            P("dp", "tensor"),
            P(("dp", "tensor")),
            P("dp", "tensor"),
            P("dp", "tensor"),
            P(("dp", "tensor"), None),
            P("dp", "tensor"),
            P(None, "tensor"),
            P(),
            P("tensor"),
            P("tensor"),
            P("tensor"),
            P("tensor"),
            P("dp", "tensor"),
        ),
        check_vma=False,
    )
```

profile of v0, /device:TPU:0, one launch (start us, length us, event | category | flops | bytes accessed | tf_op | source)
XLA Modules:
  0.0 1484.7 jit_solution(13027196084673750495)
XLA Ops:
  13.2 1059.6 %while.42 = (s32[]{:T(128)}, bf16[4096,256]{1,0:T(8,128)(2,1)}, f32[4096,256]{1,0:T(8,128)}, f32[1024,512]{1,0:T(8,128)}, f32[1024,512]{1,0:T(8,128)}, /*index=5...) while((s32[]{:T(128)}, bf16[4096,256]{1,0:T(8,128)(2,1)}, ...), condition=%wide.region_37.38_spmd.clone, body=%wide.region_0.37_spmd.clone.sunk | while | flops 44807921664 | bytes 1017131648 | solution.py:270
  22.1 22.3 %all-gather.3 = bf16[8,1,128]{2,1,0:T(2,128)(2,1)S(1)} all-gather(bf16[1,1,128]{2,1,0:T(2,128)(2,1)S(1)} %bitcast.471), channel_id=1, replica_groups=mesh['dp'=8,'tensor'=4] {'dp'}, dimensions={0}, use_global_device_ids=true | all-gather | bytes 2304 | tf_op jit(solution)/shard_map/while/body/eval_jaxpr/all_gather | solution.py:135
  44.5 26.4 %all_gather.106 = bf16[1024,8]{0,1:T(8,128)(2,1)S(1)} all-gather(bf16[128,8]{0,1:T(8,128)(2,1)S(1)} %get-tuple-element.1370), channel_id=1, replica_groups=mesh['dp'=8,'tensor'=4] {'dp'}, dimensions={0}, use_global_device_ids=true | all-gather | bytes 18432 | tf_op jit(solution)/shard_map/while/body/eval_jaxpr/all_gather | solution.py:139
  72.8 31.3 %all_gather.105 = bf16[1024,256]{1,0:T(8,128)(2,1)S(1)} all-gather(bf16[128,256]{1,0:T(8,128)(2,1)S(1)} %get-tuple-element.1373), channel_id=1, replica_groups=mesh['dp'=8,'tensor'=4] {'dp'}, dimensions={0}, use_global_device_ids=true | all-gather | bytes 589824 | tf_op jit(solution)/shard_map/while/body/eval_jaxpr/all_gather | solution.py:138
  176.9 20.4 %fusion.380 = f32[8,256,8,64]{1,3,2,0:T(8,128)} fusion(f32[8,8,64,256]{3,2,1,0:T(8,128)S(1)} %fusion.378, f32[8,256,8]{1,2,0:T(8,128)S(1)} %get-tuple-element.1222, f32[8,8,256]{2,1,0:T(8,128)S(1)} %get-tuple-element.1221, f32[8,256,256]{2,1,0:T(8,128)S(1)} %fusion.379, pred[256,256]{1,0:T(8,128)(4,1)S(1)} %iota_compare_fusion.7, ...), kind=kOutput, calls=%fused_computation.51.clone.1 | convolution fusion | flops 3236954112 | bytes 14942208 | tf_op jit(solution)/shard_map/while/body/eval_jaxpr/jvp(bhqs,bshp->bqhp)/dot_general | solution.py:34
  247.6 13.3 multiply_reduce_fusion.26
  308.1 25.1 %fusion.381 = (f32[8,8,256]{2,1,0:T(8,128)}, f32[8,8,256]{2,1,0:T(8,128)}, f32[8,256,256]{2,1,0:T(8,128)}) fusion(f32[8,8,256]{2,1,0:T(8,128)S(1)} %get-tuple-element.1221, f32[8,256,256]{2,1,0:T(8,128)S(1)} %copy-done.27, pred[256,256]{1,0:T(8,128)(4,1)S(1)} %copy-done.40, f32[8,256,8,64]{1,3,2,0:T(8,128)S(1)} %copy-done.1, ...), kind=kOutput, calls=%fused_computation.12.clone.1 | convolution fusion | flops 3259465728 | bytes 12910592 | tf_op jit(solution)/shard_map/while/body/eval_jaxpr/transpose(jvp(bhqs,bshp->bqhp))/dot_general | solution.py:34
  344.6 20.5 %reduce-window.49 = f32[8,8,2,128]{3,1,2,0:T(8,128)S(1)} reduce-window(f32[8,8,2,128]{3,1,2,0:T(8,128)} %fusion.386, f32[]{:T(128)} %constant.161.clone.1..sunk), window={size=1x1x1x128 pad=0_0x0_0x0_0x0_127}, to_apply=%region_17.17 | reduce-window | flops 2080768 | bytes 131076 | tf_op jit(solution)/shard_map/reduce-window.18
  365.3 18.4 %multiply_reduce_fusion.29 = (f32[8,256,8]{1,2,0:T(8,128)S(1)}, f32[8,256,8,64]{1,3,2,0:T(8,128)}) fusion(f32[8,256,8,64]{1,3,2,0:T(8,128)} %copy.347, f32[8,256,8]{1,2,0:T(8,128)S(1)} %bitcast.432, f32[8,8,256]{2,1,0:T(8,128)S(1)} %get-tuple-element.1221, f32[8,256,256]{2,1,0:T(8,128)} %copy-done.26, pred[256,256]{1,0:T(8,128)(4,1)} %copy-done.39, ...), kind=kOutput, calls=%fused_computation.61.clone.1 | convolution fusion | flops 3239034880 | bytes 19202048 | tf_op jit(solution)/shard_map/while/body/eval_jaxpr/transpose(jvp(bhqs,bshp->bqhp))/dot_general | solution.py:34
  488.4 27.1 %all-to-all-done = bf16[4,512,512]{1,2,0:T(8,128)(2,1)} async-done(((bf16[4,512,512]{1,2,0:T(8,128)(2,1)}), bf16[4,512,512]{1,2,0:T(8,128)(2,1)}, u32[]{:S(2)}, u32[]{:S(2)}) %all-to-all-start) | async-done | bytes 2097184 | tf_op jit(solution)/shard_map/while/body/eval_jaxpr/all_to_all | solution.py:167
  554.1 16.3 %all-gather.3 = bf16[8,1,128]{2,1,0:T(2,128)(2,1)S(1)} all-gather(bf16[1,1,128]{2,1,0:T(2,128)(2,1)S(1)} %bitcast.471), channel_id=1, replica_groups=mesh['dp'=8,'tensor'=4] {'dp'}, dimensions={0}, use_global_device_ids=true | all-gather | bytes 2304 | tf_op jit(solution)/shard_map/while/body/eval_jaxpr/all_gather | solution.py:135
  570.6 26.3 %all_gather.106 = bf16[1024,8]{0,1:T(8,128)(2,1)S(1)} all-gather(bf16[128,8]{0,1:T(8,128)(2,1)S(1)} %get-tuple-element.1370), channel_id=1, replica_groups=mesh['dp'=8,'tensor'=4] {'dp'}, dimensions={0}, use_global_device_ids=true | all-gather | bytes 18432 | tf_op jit(solution)/shard_map/while/body/eval_jaxpr/all_gather | solution.py:139
  598.8 31.3 %all_gather.105 = bf16[1024,256]{1,0:T(8,128)(2,1)S(1)} all-gather(bf16[128,256]{1,0:T(8,128)(2,1)S(1)} %get-tuple-element.1373), channel_id=1, replica_groups=mesh['dp'=8,'tensor'=4] {'dp'}, dimensions={0}, use_global_device_ids=true | all-gather | bytes 589824 | tf_op jit(solution)/shard_map/while/body/eval_jaxpr/all_gather | solution.py:138
  702.1 20.4 %fusion.380 = f32[8,256,8,64]{1,3,2,0:T(8,128)} fusion(f32[8,8,64,256]{3,2,1,0:T(8,128)S(1)} %fusion.378, f32[8,256,8]{1,2,0:T(8,128)S(1)} %get-tuple-element.1222, f32[8,8,256]{2,1,0:T(8,128)S(1)} %get-tuple-element.1221, f32[8,256,256]{2,1,0:T(8,128)S(1)} %fusion.379, pred[256,256]{1,0:T(8,128)(4,1)S(1)} %iota_compare_fusion.7, ...), kind=kOutput, calls=%fused_computation.51.clone.1 | convolution fusion | flops 3236954112 | bytes 14942208 | tf_op jit(solution)/shard_map/while/body/eval_jaxpr/jvp(bhqs,bshp->bqhp)/dot_general | solution.py:34
  833.4 25.1 %fusion.381 = (f32[8,8,256]{2,1,0:T(8,128)}, f32[8,8,256]{2,1,0:T(8,128)}, f32[8,256,256]{2,1,0:T(8,128)}) fusion(f32[8,8,256]{2,1,0:T(8,128)S(1)} %get-tuple-element.1221, f32[8,256,256]{2,1,0:T(8,128)S(1)} %copy-done.27, pred[256,256]{1,0:T(8,128)(4,1)S(1)} %copy-done.40, f32[8,256,8,64]{1,3,2,0:T(8,128)S(1)} %copy-done.1, ...), kind=kOutput, calls=%fused_computation.12.clone.1 | convolution fusion | flops 3259465728 | bytes 12910592 | tf_op jit(solution)/shard_map/while/body/eval_jaxpr/transpose(jvp(bhqs,bshp->bqhp))/dot_general | solution.py:34
  869.9 20.5 %reduce-window.49 = f32[8,8,2,128]{3,1,2,0:T(8,128)S(1)} reduce-window(f32[8,8,2,128]{3,1,2,0:T(8,128)} %fusion.386, f32[]{:T(128)} %constant.161.clone.1..sunk), window={size=1x1x1x128 pad=0_0x0_0x0_0x0_127}, to_apply=%region_17.17 | reduce-window | flops 2080768 | bytes 131076 | tf_op jit(solution)/shard_map/reduce-window.18
  890.6 18.4 %multiply_reduce_fusion.29 = (f32[8,256,8]{1,2,0:T(8,128)S(1)}, f32[8,256,8,64]{1,3,2,0:T(8,128)}) fusion(f32[8,256,8,64]{1,3,2,0:T(8,128)} %copy.347, f32[8,256,8]{1,2,0:T(8,128)S(1)} %bitcast.432, f32[8,8,256]{2,1,0:T(8,128)S(1)} %get-tuple-element.1221, f32[8,256,256]{2,1,0:T(8,128)} %copy-done.26, pred[256,256]{1,0:T(8,128)(4,1)} %copy-done.39, ...), kind=kOutput, calls=%fused_computation.61.clone.1 | convolution fusion | flops 3239034880 | bytes 19202048 | tf_op jit(solution)/shard_map/while/body/eval_jaxpr/transpose(jvp(bhqs,bshp->bqhp))/dot_general | solution.py:34
  1016.7 24.3 %all-to-all-done = bf16[4,512,512]{1,2,0:T(8,128)(2,1)} async-done(((bf16[4,512,512]{1,2,0:T(8,128)(2,1)}), bf16[4,512,512]{1,2,0:T(8,128)(2,1)}, u32[]{:S(2)}, u32[]{:S(2)}) %all-to-all-start) | async-done | bytes 2097184 | tf_op jit(solution)/shard_map/while/body/eval_jaxpr/all_to_all | solution.py:167
  1076.1 37.1 %all-reduce.25 = (f32[1024]{0:T(1024)S(1)}, f32[5,256]{1,0:T(8,128)}) all-reduce(f32[1024]{0:T(1024)S(1)} %copy-done.71, f32[5,256]{1,0:T(8,128)S(1)} %copy-done.59), channel_id=3, replica_groups=mesh['dp'=8,'tensor'=4] {'dp','tensor'}, use_global_device_ids=true, to_apply=%region_38.39.clone | all-reduce | flops 2304 | bytes 18432
  1113.8 37.3 %all-reduce.26 = (f32[5,512]{1,0:T(8,128)}, f32[8]{0:T(128)}, f32[8]{0:T(128)}, f32[8]{0:T(128)}, f32[512]{0:T(512)}) all-reduce(f32[5,512]{1,0:T(8,128)S(1)} %copy-done.50, f32[8]{0:T(128)S(1)} %copy-done.89, f32[8]{0:T(128)S(1)} %copy-done.92, f32[8]{0:T(128)S(1)} %copy-done.86, ...), channel_id=1, replica_groups=mesh['dp'=8,'tensor'=4] {'dp'}, use_global_device_ids=true, to_apply=%region_43.44 | all-reduce | flops 3096 | bytes 24768 | tf_op jit(solution)/shard_map/psum | solution.py:297
  1151.1 115.0 %reduce-scatter.11.cloned.1.call-done = f32[32,256]{1,0:T(8,128)} async-done(((f32[1024,256]{1,0:T(8,128)}), f32[32,256]{1,0:T(8,128)}) %reduce-scatter.11.cloned.1.call-update) | async-done | bytes 32784 | tf_op jit(solution)/shard_map/reduce_scatter | solution.py:294
  1266.1 68.2 %reduce-scatter.7.cloned.1.call-done = f32[128,512]{1,0:T(8,128)} async-done(((f32[1024,512]{1,0:T(8,128)}), f32[128,512]{1,0:T(8,128)}) %reduce-scatter.7.cloned.1.call-update) | async-done | bytes 262160 | tf_op jit(solution)/shard_map/reduce_scatter | solution.py:288
  1334.3 71.3 %reduce-scatter.9.cloned.1.call-done = f32[128,512]{1,0:T(8,128)} async-done(((f32[1024,512]{1,0:T(8,128)}), f32[128,512]{1,0:T(8,128)}) %reduce-scatter.9.cloned.1.call-update) | async-done | bytes 262160 | tf_op jit(solution)/shard_map/reduce_scatter | solution.py:289
  1405.6 71.5 %reduce-scatter.15.cloned.1.call-done = f32[128,512]{1,0:T(8,128)} async-done(((f32[1024,512]{1,0:T(8,128)}), f32[128,512]{1,0:T(8,128)}) %reduce-scatter.15.cloned.1.call-update) | async-done | bytes 262160 | tf_op jit(solution)/shard_map/reduce_scatter | solution.py:291
  (660 shorter events, 675.7 us)
Async XLA Ops:
  13.5 90.7 %all-gather.19.cloned.1.call-start = ((), (), s32[]{:S(2)}) async-start(), calls=%async_computation.17 | async-start | bytes 1179648 | tf_op jit(solution)/shard_map/while/body/eval_jaxpr/all_gather | solution.py:140
  14.2 90.0 %all-gather.11.cloned.1.call-start = ((), (), s32[]{:S(2)}) async-start(), calls=%async_computation.13 | async-start | bytes 5242880 | tf_op jit(solution)/shard_map/while/body/eval_jaxpr/all_gather | solution.py:143
  16.5 120.6 %all-gather.13.cloned.1.call-start = ((), (), s32[]{:S(2)}) async-start(), calls=%async_computation.14 | async-start | bytes 1179648 | tf_op jit(solution)/shard_map/while/body/eval_jaxpr/all_gather | solution.py:137
  17.3 194.8 %all-gather.15.cloned.1.call-start = ((), (), s32[]{:S(2)}) async-start(), calls=%async_computation.15 | async-start | bytes 1179648 | tf_op jit(solution)/shard_map/while/body/eval_jaxpr/all_gather | solution.py:136
  17.9 213.8 %all-gather.17.cloned.1.call-start = ((), (), s32[]{:S(2)}) async-start(), calls=%async_computation.16 | async-start | bytes 5242880 | tf_op jit(solution)/shard_map/while/body/eval_jaxpr/all_gather | solution.py:180
  22.0 493.5 %all-gather.21.cloned.1.call-start = ((), (), s32[]{:S(2)}) async-start(), calls=%async_computation.18 | async-start | bytes 5242880 | tf_op jit(solution)/shard_map/while/body/eval_jaxpr/all_gather | solution.py:168
  44.5 203.1 %copy-start.55 = (f32[512]{0:T(512)}, f32[512]{0:T(512)S(1)}, u32[]{:S(2)}) copy-start(f32[512]{0:T(512)S(1)} %mul.1764) | copy-start | bytes 6148 | tf_op jit(solution)/shard_map/while
  104.1 438.3 %reduce-scatter.17.cloned.1.call-start = ((), (), s32[]{:S(2)}) async-start(), calls=%async_computation.19 | async-start | bytes 5242880 | tf_op jit(solution)/shard_map/while/body/eval_jaxpr/reduce_scatter | solution.py:232
  469.9 45.7 %all-to-all-start = ((bf16[4,512,512]{1,2,0:T(8,128)(2,1)}), bf16[4,512,512]{1,2,0:T(8,128)(2,1)}, u32[]{:S(2)}, u32[]{:S(2)}) async-start(bf16[4,512,512]{1,2,0:T(8,128)(2,1)} %copy.353), calls=%async_computation | async-start | bytes 4194304 | tf_op jit(solution)/shard_map/while/body/eval_jaxpr/all_to_all | solution.py:167
  521.8 18.1 %all-to-all-start.1 = ((bf16[512,4,256]{2,0,1:T(8,128)(2,1)}), bf16[512,4,256]{2,0,1:T(8,128)(2,1)S(1)}, u32[]{:S(2)}, u32[]{:S(2)}) async-start(bf16[512,4,256]{2,0,1:T(8,128)(2,1)} %bitcast.423), calls=%async_computation.1 | async-start | bytes 2097152 | tf_op jit(solution)/shard_map/while/body/eval_jaxpr/all_to_all | solution.py:169
  545.5 84.6 %all-gather.19.cloned.1.call-start = ((), (), s32[]{:S(2)}) async-start(), calls=%async_computation.17 | async-start | bytes 1179648 | tf_op jit(solution)/shard_map/while/body/eval_jaxpr/all_gather | solution.py:140
  546.2 84.0 %all-gather.11.cloned.1.call-start = ((), (), s32[]{:S(2)}) async-start(), calls=%async_computation.13 | async-start | bytes 5242880 | tf_op jit(solution)/shard_map/while/body/eval_jaxpr/all_gather | solution.py:143
  548.6 113.9 %all-gather.13.cloned.1.call-start = ((), (), s32[]{:S(2)}) async-start(), calls=%async_computation.14 | async-start | bytes 1179648 | tf_op jit(solution)/shard_map/while/body/eval_jaxpr/all_gather | solution.py:137
  549.2 188.1 %all-gather.15.cloned.1.call-start = ((), (), s32[]{:S(2)}) async-start(), calls=%async_computation.15 | async-start | bytes 1179648 | tf_op jit(solution)/shard_map/while/body/eval_jaxpr/all_gather | solution.py:136
  549.9 207.1 %all-gather.17.cloned.1.call-start = ((), (), s32[]{:S(2)}) async-start(), calls=%async_computation.16 | async-start | bytes 5242880 | tf_op jit(solution)/shard_map/while/body/eval_jaxpr/all_gather | solution.py:180
  554.1 486.9 %all-gather.21.cloned.1.call-start = ((), (), s32[]{:S(2)}) async-start(), calls=%async_computation.18 | async-start | bytes 5242880 | tf_op jit(solution)/shard_map/while/body/eval_jaxpr/all_gather | solution.py:168
  630.1 437.7 %reduce-scatter.17.cloned.1.call-start = ((), (), s32[]{:S(2)}) async-start(), calls=%async_computation.19 | async-start | bytes 5242880 | tf_op jit(solution)/shard_map/while/body/eval_jaxpr/reduce_scatter | solution.py:232
  995.2 45.8 %all-to-all-start = ((bf16[4,512,512]{1,2,0:T(8,128)(2,1)}), bf16[4,512,512]{1,2,0:T(8,128)(2,1)}, u32[]{:S(2)}, u32[]{:S(2)}) async-start(bf16[4,512,512]{1,2,0:T(8,128)(2,1)} %copy.353), calls=%async_computation | async-start | bytes 4194304 | tf_op jit(solution)/shard_map/while/body/eval_jaxpr/all_to_all | solution.py:167
  1047.3 18.1 %all-to-all-start.1 = ((bf16[512,4,256]{2,0,1:T(8,128)(2,1)}), bf16[512,4,256]{2,0,1:T(8,128)(2,1)S(1)}, u32[]{:S(2)}, u32[]{:S(2)}) async-start(bf16[512,4,256]{2,0,1:T(8,128)(2,1)} %bitcast.423), calls=%async_computation.1 | async-start | bytes 2097152 | tf_op jit(solution)/shard_map/while/body/eval_jaxpr/all_to_all | solution.py:169
  1072.8 78.3 %reduce-scatter.13.cloned.1.call-start = ((), (), s32[]{:S(2)}) async-start(), calls=%async_computation.11 | async-start | bytes 36864 | tf_op jit(solution)/shard_map/reduce_scatter | solution.py:290
  1073.4 192.7 %reduce-scatter.11.cloned.1.call-start = ((), (), s32[]{:S(2)}) async-start(), calls=%async_computation.10 | async-start | bytes 1081344 | tf_op jit(solution)/shard_map/reduce_scatter | solution.py:294
  1074.0 260.3 %reduce-scatter.7.cloned.1.call-start = ((), (), s32[]{:S(2)}) async-start(), calls=%async_computation.8 | async-start | bytes 2359296 | tf_op jit(solution)/shard_map/reduce_scatter | solution.py:288
  1074.6 331.0 %reduce-scatter.9.cloned.1.call-start = ((), (), s32[]{:S(2)}) async-start(), calls=%async_computation.9 | async-start | bytes 2359296 | tf_op jit(solution)/shard_map/reduce_scatter | solution.py:289
  1075.3 401.8 %reduce-scatter.15.cloned.1.call-start = ((), (), s32[]{:S(2)}) async-start(), calls=%async_computation.12 | async-start | bytes 2359296 | tf_op jit(solution)/shard_map/reduce_scatter | solution.py:291
  (189 other events, 2883.9 us)
Sparse Core Ops, SparseCore 0:
  16.4 42.9 all-gather.18
  61.0 33.5 all-gather.10
  96.7 40.3 all-gather.12
  139.1 38.9 all-gather.14
  179.5 33.7 all-gather.16
  214.7 34.9 all-gather.20
  466.0 58.0 reduce-scatter.16
  548.4 36.5 all-gather.18
  586.6 33.5 all-gather.10
  622.2 40.2 all-gather.12
  664.6 38.9 all-gather.14
  705.0 33.7 all-gather.16
  740.4 34.9 all-gather.20
  991.3 58.0 reduce-scatter.16
Sparse Core Ops, SparseCore 1:
  1077.0 50.9 reduce-scatter.12
  1130.7 135.4 reduce-scatter.10
  1270.1 64.1 reduce-scatter.6
  1338.4 67.1 reduce-scatter.8
  1409.7 67.3 reduce-scatter.14
where the time goes:
time: 1490 us; the launch traced here: 1480 us
  waiting for transfers between devices  426 us (29%)
  matrix products  400 us (27%)
  blocking collectives  256 us (17%)
  other arithmetic  207 us (14%)
  local copies, waits for them, and re-layouts  157 us (11%)
  starting transfers between devices  17.3 us (1%)
  between operations  16 us (1%)
    dot_general x6, matrix products, group_scan(): jnp.einsum('bhqs,bshp->bqhp', intersection[:, None] * decay_grid, weighte...  128 us
    reduce_scatter x1, waiting for transfers between devices, per_device(): lax.psum_scatter(acc_shared, ('dp', 'tensor'), scatter_dimension=0, tiled...  115 us
    another operation x16, other arithmetic  74.9 us
    reduce_scatter x1, waiting for transfers between devices, per_device(): lax.psum_scatter(acc_out, 'dp', scatter_dimension=0, tiled=True)  71.5 us
    reduce_scatter x1, waiting for transfers between devices, per_device(): lax.psum_scatter(acc_value, 'dp', scatter_dimension=0, tiled=True)  71.3 us
    reduce_scatter x1, waiting for transfers between devices, per_device(): lax.psum_scatter(acc_gate, 'dp', scatter_dimension=0, tiled=True)  68.2 us
    all_gather x2, blocking collectives, micro_step(): lax.all_gather(w_bc, 'dp', axis=0, tiled=True)  62.6 us
    reshape x8, local copies, waits for them, and re-layouts, group_scan(): values = values.reshape(blocks, GROUP, head_count, head_width)  57.2 us
  transfers between devices with their start and end apart: 23, of which 10 were waited for; matrix products, arithmetic and copies ran while one was open for 49% of the time, Pallas kernels for 0%

commit v1 on v0

--- a/solution.py
+++ b/solution.py
@@ -164,7 +164,15 @@
         squares = lax.psum(jnp.sum(mixed_out * mixed_out, -1), "tensor")
         inverse_gate = lax.rsqrt(squares / inner_all + epsilon)[:, None]
         normed_out = (mixed_out * inverse_gate * gate_gain).astype(jnp.bfloat16)
-        row_block = lax.all_to_all(normed_out, "tensor", split_axis=0, concat_axis=1, tiled=True)
+        row_block = jnp.concatenate(
+            lax.all_to_all(
+                jnp.stack(jnp.split(normed_out, lax.axis_size("tensor"), axis=0), axis=0),
+                "tensor",
+                0,
+                0,
+            ),
+            axis=1,
+        )
         out_full = lax.all_gather(out_weight, "tensor", axis=1, tiled=True)
         branch_rows = lax.all_to_all(
             against(row_block, out_full).astype(jnp.bfloat16),

time: 1490 us -> 1490 us (level)
    another operation x16 -> x18, other arithmetic: 74.9 us -> 78 us
  transfers between devices with their start and end apart: 23 -> 23, of which waited for: 10 -> 10; matrix products, arithmetic and copies ran while one was open for 49% -> 50% of each run, Pallas kernels for 0% -> 0%
where the time goes in v1:
time: 1490 us; the launch traced here: 1480 us
  waiting for transfers between devices  424 us (28%)
  matrix products  400 us (27%)
  blocking collectives  256 us (17%)
  other arithmetic  210 us (14%)
  local copies, waits for them, and re-layouts  157 us (11%)
  between operations  15.9 us (1%)
  starting transfers between devices  15.7 us (1%)
    dot_general x6, matrix products, group_scan(): jnp.einsum('bhqs,bshp->bqhp', intersection[:, None] * decay_grid, weighte...  128 us
    reduce_scatter x1, waiting for transfers between devices, per_device(): lax.psum_scatter(acc_shared, ('dp', 'tensor'), scatter_dimension=0, tiled...  115 us
    another operation x16, other arithmetic  74.8 us
    reduce_scatter x1, waiting for transfers between devices, per_device(): lax.psum_scatter(acc_value, 'dp', scatter_dimension=0, tiled=True)  71.6 us
    reduce_scatter x1, waiting for transfers between devices, per_device(): lax.psum_scatter(acc_out, 'dp', scatter_dimension=0, tiled=True)  71.2 us
    reduce_scatter x1, waiting for transfers between devices, per_device(): lax.psum_scatter(acc_gate, 'dp', scatter_dimension=0, tiled=True)  68.2 us
    all_gather x2, blocking collectives, micro_step(): lax.all_gather(w_bc, 'dp', axis=0, tiled=True)  62.5 us
    reshape x8, local copies, waits for them, and re-layouts, group_scan(): values = values.reshape(blocks, GROUP, head_count, head_width)  57.5 us
  transfers between devices with their start and end apart: 23, of which 10 were waited for; matrix products, arithmetic and copies ran while one was open for 50% of the time, Pallas kernels for 0%

profile of v1, /device:TPU:0, one launch (start us, length us, event | category | flops | bytes accessed | tf_op | source)
XLA Modules:
  0.0 1484.5 jit_solution(5973517461454493193)
XLA Ops:
  13.2 1059.2 %while.42 = (s32[]{:T(128)}, bf16[4096,256]{1,0:T(8,128)(2,1)}, f32[4096,256]{1,0:T(8,128)}, f32[1024,512]{1,0:T(8,128)}, f32[1024,512]{1,0:T(8,128)}, /*index=5...) while((s32[]{:T(128)}, bf16[4096,256]{1,0:T(8,128)(2,1)}, ...), condition=%wide.region_37.38_spmd.clone, body=%wide.region_0.37_spmd.clone.sunk | while | flops 44811067392 | bytes 1033908864 | solution.py:278
  22.0 22.3 %all-gather.3 = bf16[8,1,128]{2,1,0:T(2,128)(2,1)S(1)} all-gather(bf16[1,1,128]{2,1,0:T(2,128)(2,1)S(1)} %bitcast.480), channel_id=1, replica_groups=mesh['dp'=8,'tensor'=4] {'dp'}, dimensions={0}, use_global_device_ids=true | all-gather | bytes 2304 | tf_op jit(solution)/shard_map/while/body/eval_jaxpr/all_gather | solution.py:135
  44.4 26.4 %all_gather.106 = bf16[1024,8]{0,1:T(8,128)(2,1)S(1)} all-gather(bf16[128,8]{0,1:T(8,128)(2,1)S(1)} %get-tuple-element.1382), channel_id=1, replica_groups=mesh['dp'=8,'tensor'=4] {'dp'}, dimensions={0}, use_global_device_ids=true | all-gather | bytes 18432 | tf_op jit(solution)/shard_map/while/body/eval_jaxpr/all_gather | solution.py:139
  72.7 31.3 %all_gather.105 = bf16[1024,256]{1,0:T(8,128)(2,1)S(1)} all-gather(bf16[128,256]{1,0:T(8,128)(2,1)S(1)} %get-tuple-element.1385), channel_id=1, replica_groups=mesh['dp'=8,'tensor'=4] {'dp'}, dimensions={0}, use_global_device_ids=true | all-gather | bytes 589824 | tf_op jit(solution)/shard_map/while/body/eval_jaxpr/all_gather | solution.py:138
  176.9 20.4 %fusion.380 = f32[8,256,8,64]{1,3,2,0:T(8,128)} fusion(f32[8,8,64,256]{3,2,1,0:T(8,128)S(1)} %fusion.378, f32[8,256,8]{1,2,0:T(8,128)S(1)} %get-tuple-element.1230, f32[8,8,256]{2,1,0:T(8,128)S(1)} %get-tuple-element.1229, f32[8,256,256]{2,1,0:T(8,128)S(1)} %fusion.379, pred[256,256]{1,0:T(8,128)(4,1)S(1)} %iota_compare_fusion.7, ...), kind=kOutput, calls=%fused_computation.51.clone.1 | convolution fusion | flops 3236954112 | bytes 14942208 | tf_op jit(solution)/shard_map/while/body/eval_jaxpr/jvp(bhqs,bshp->bqhp)/dot_general | solution.py:34
  247.7 13.3 multiply_reduce_fusion.26
  308.0 25.1 %fusion.381 = (f32[8,8,256]{2,1,0:T(8,128)}, f32[8,8,256]{2,1,0:T(8,128)}, f32[8,256,256]{2,1,0:T(8,128)}) fusion(f32[8,8,256]{2,1,0:T(8,128)S(1)} %get-tuple-element.1229, f32[8,256,256]{2,1,0:T(8,128)S(1)} %copy-done.28, pred[256,256]{1,0:T(8,128)(4,1)S(1)} %copy-done.41, f32[8,256,8,64]{1,3,2,0:T(8,128)S(1)} %copy-done.1, ...), kind=kOutput, calls=%fused_computation.12.clone.1 | convolution fusion | flops 3259465728 | bytes 12910592 | tf_op jit(solution)/shard_map/while/body/eval_jaxpr/transpose(jvp(bhqs,bshp->bqhp))/dot_general | solution.py:34
  344.5 20.5 %reduce-window.49 = f32[8,8,2,128]{3,1,2,0:T(8,128)S(1)} reduce-window(f32[8,8,2,128]{3,1,2,0:T(8,128)} %fusion.386, f32[]{:T(128)} %constant.161.clone.1..sunk), window={size=1x1x1x128 pad=0_0x0_0x0_0x0_127}, to_apply=%region_17.17 | reduce-window | flops 2080768 | bytes 131076 | tf_op jit(solution)/shard_map/reduce-window.18
  365.3 18.4 %multiply_reduce_fusion.29 = (f32[8,256,8]{1,2,0:T(8,128)S(1)}, f32[8,256,8,64]{1,3,2,0:T(8,128)}) fusion(f32[8,256,8,64]{1,3,2,0:T(8,128)} %copy.347, f32[8,256,8]{1,2,0:T(8,128)S(1)} %bitcast.440, f32[8,8,256]{2,1,0:T(8,128)S(1)} %get-tuple-element.1229, f32[8,256,256]{2,1,0:T(8,128)} %copy-done.27, pred[256,256]{1,0:T(8,128)(4,1)} %copy-done.40, ...), kind=kOutput, calls=%fused_computation.61.clone.1 | convolution fusion | flops 3239034880 | bytes 19202048 | tf_op jit(solution)/shard_map/while/body/eval_jaxpr/transpose(jvp(bhqs,bshp->bqhp))/dot_general | solution.py:34
  487.1 25.7 %all-to-all-done = bf16[4,512,512]{2,1,0:T(8,128)(2,1)S(1)} async-done(((bf16[4,512,512]{2,1,0:T(8,128)(2,1)}), bf16[4,512,512]{2,1,0:T(8,128)(2,1)S(1)}, u32[]{:S(2)}, u32[]{:S(2)}) %all-to-all-start) | async-done | bytes 2097184 | tf_op jit(solution)/shard_map/while/body/eval_jaxpr/all_to_all | solution.py:168
  553.8 16.3 %all-gather.3 = bf16[8,1,128]{2,1,0:T(2,128)(2,1)S(1)} all-gather(bf16[1,1,128]{2,1,0:T(2,128)(2,1)S(1)} %bitcast.480), channel_id=1, replica_groups=mesh['dp'=8,'tensor'=4] {'dp'}, dimensions={0}, use_global_device_ids=true | all-gather | bytes 2304 | tf_op jit(solution)/shard_map/while/body/eval_jaxpr/all_gather | solution.py:135
  570.2 26.4 %all_gather.106 = bf16[1024,8]{0,1:T(8,128)(2,1)S(1)} all-gather(bf16[128,8]{0,1:T(8,128)(2,1)S(1)} %get-tuple-element.1382), channel_id=1, replica_groups=mesh['dp'=8,'tensor'=4] {'dp'}, dimensions={0}, use_global_device_ids=true | all-gather | bytes 18432 | tf_op jit(solution)/shard_map/while/body/eval_jaxpr/all_gather | solution.py:139
  598.5 31.2 %all_gather.105 = bf16[1024,256]{1,0:T(8,128)(2,1)S(1)} all-gather(bf16[128,256]{1,0:T(8,128)(2,1)S(1)} %get-tuple-element.1385), channel_id=1, replica_groups=mesh['dp'=8,'tensor'=4] {'dp'}, dimensions={0}, use_global_device_ids=true | all-gather | bytes 589824 | tf_op jit(solution)/shard_map/while/body/eval_jaxpr/all_gather | solution.py:138
  701.8 20.4 %fusion.380 = f32[8,256,8,64]{1,3,2,0:T(8,128)} fusion(f32[8,8,64,256]{3,2,1,0:T(8,128)S(1)} %fusion.378, f32[8,256,8]{1,2,0:T(8,128)S(1)} %get-tuple-element.1230, f32[8,8,256]{2,1,0:T(8,128)S(1)} %get-tuple-element.1229, f32[8,256,256]{2,1,0:T(8,128)S(1)} %fusion.379, pred[256,256]{1,0:T(8,128)(4,1)S(1)} %iota_compare_fusion.7, ...), kind=kOutput, calls=%fused_computation.51.clone.1 | convolution fusion | flops 3236954112 | bytes 14942208 | tf_op jit(solution)/shard_map/while/body/eval_jaxpr/jvp(bhqs,bshp->bqhp)/dot_general | solution.py:34
  833.1 25.1 %fusion.381 = (f32[8,8,256]{2,1,0:T(8,128)}, f32[8,8,256]{2,1,0:T(8,128)}, f32[8,256,256]{2,1,0:T(8,128)}) fusion(f32[8,8,256]{2,1,0:T(8,128)S(1)} %get-tuple-element.1229, f32[8,256,256]{2,1,0:T(8,128)S(1)} %copy-done.28, pred[256,256]{1,0:T(8,128)(4,1)S(1)} %copy-done.41, f32[8,256,8,64]{1,3,2,0:T(8,128)S(1)} %copy-done.1, ...), kind=kOutput, calls=%fused_computation.12.clone.1 | convolution fusion | flops 3259465728 | bytes 12910592 | tf_op jit(solution)/shard_map/while/body/eval_jaxpr/transpose(jvp(bhqs,bshp->bqhp))/dot_general | solution.py:34
  869.6 20.5 %reduce-window.49 = f32[8,8,2,128]{3,1,2,0:T(8,128)S(1)} reduce-window(f32[8,8,2,128]{3,1,2,0:T(8,128)} %fusion.386, f32[]{:T(128)} %constant.161.clone.1..sunk), window={size=1x1x1x128 pad=0_0x0_0x0_0x0_127}, to_apply=%region_17.17 | reduce-window | flops 2080768 | bytes 131076 | tf_op jit(solution)/shard_map/reduce-window.18
  890.3 18.4 %multiply_reduce_fusion.29 = (f32[8,256,8]{1,2,0:T(8,128)S(1)}, f32[8,256,8,64]{1,3,2,0:T(8,128)}) fusion(f32[8,256,8,64]{1,3,2,0:T(8,128)} %copy.347, f32[8,256,8]{1,2,0:T(8,128)S(1)} %bitcast.440, f32[8,8,256]{2,1,0:T(8,128)S(1)} %get-tuple-element.1229, f32[8,256,256]{2,1,0:T(8,128)} %copy-done.27, pred[256,256]{1,0:T(8,128)(4,1)} %copy-done.40, ...), kind=kOutput, calls=%fused_computation.61.clone.1 | convolution fusion | flops 3239034880 | bytes 19202048 | tf_op jit(solution)/shard_map/while/body/eval_jaxpr/transpose(jvp(bhqs,bshp->bqhp))/dot_general | solution.py:34
  1015.1 23.0 %all-to-all-done = bf16[4,512,512]{2,1,0:T(8,128)(2,1)S(1)} async-done(((bf16[4,512,512]{2,1,0:T(8,128)(2,1)}), bf16[4,512,512]{2,1,0:T(8,128)(2,1)S(1)}, u32[]{:S(2)}, u32[]{:S(2)}) %all-to-all-start) | async-done | bytes 2097184 | tf_op jit(solution)/shard_map/while/body/eval_jaxpr/all_to_all | solution.py:168
  1075.8 37.0 %all-reduce.25 = (f32[1024]{0:T(1024)S(1)}, f32[5,256]{1,0:T(8,128)}) all-reduce(f32[1024]{0:T(1024)S(1)} %copy-done.72, f32[5,256]{1,0:T(8,128)S(1)} %copy-done.60), channel_id=3, replica_groups=mesh['dp'=8,'tensor'=4] {'dp','tensor'}, use_global_device_ids=true, to_apply=%region_38.39.clone | all-reduce | flops 2304 | bytes 18432
  1113.4 37.4 %all-reduce.26 = (f32[5,512]{1,0:T(8,128)}, f32[8]{0:T(128)}, f32[8]{0:T(128)}, f32[8]{0:T(128)}, f32[512]{0:T(512)}) all-reduce(f32[5,512]{1,0:T(8,128)S(1)} %copy-done.51, f32[8]{0:T(128)S(1)} %copy-done.90, f32[8]{0:T(128)S(1)} %copy-done.93, f32[8]{0:T(128)S(1)} %copy-done.87, ...), channel_id=1, replica_groups=mesh['dp'=8,'tensor'=4] {'dp'}, use_global_device_ids=true, to_apply=%region_43.44 | all-reduce | flops 3096 | bytes 24768 | tf_op jit(solution)/shard_map/psum | solution.py:305
  1150.8 115.1 %reduce-scatter.11.cloned.1.call-done = f32[32,256]{1,0:T(8,128)} async-done(((f32[1024,256]{1,0:T(8,128)}), f32[32,256]{1,0:T(8,128)}) %reduce-scatter.11.cloned.1.call-update) | async-done | bytes 32784 | tf_op jit(solution)/shard_map/reduce_scatter | solution.py:302
  1265.9 68.2 %reduce-scatter.7.cloned.1.call-done = f32[128,512]{1,0:T(8,128)} async-done(((f32[1024,512]{1,0:T(8,128)}), f32[128,512]{1,0:T(8,128)}) %reduce-scatter.7.cloned.1.call-update) | async-done | bytes 262160 | tf_op jit(solution)/shard_map/reduce_scatter | solution.py:296
  1334.1 71.6 %reduce-scatter.9.cloned.1.call-done = f32[128,512]{1,0:T(8,128)} async-done(((f32[1024,512]{1,0:T(8,128)}), f32[128,512]{1,0:T(8,128)}) %reduce-scatter.9.cloned.1.call-update) | async-done | bytes 262160 | tf_op jit(solution)/shard_map/reduce_scatter | solution.py:297
  1405.7 71.2 %reduce-scatter.15.cloned.1.call-done = f32[128,512]{1,0:T(8,128)} async-done(((f32[1024,512]{1,0:T(8,128)}), f32[128,512]{1,0:T(8,128)}) %reduce-scatter.15.cloned.1.call-update) | async-done | bytes 262160 | tf_op jit(solution)/shard_map/reduce_scatter | solution.py:299
  (668 shorter events, 677.8 us)
Async XLA Ops:
  13.4 90.6 %all-gather.19.cloned.1.call-start = ((), (), s32[]{:S(2)}) async-start(), calls=%async_computation.17 | async-start | bytes 1179648 | tf_op jit(solution)/shard_map/while/body/eval_jaxpr/all_gather | solution.py:140
  14.1 90.0 %all-gather.11.cloned.1.call-start = ((), (), s32[]{:S(2)}) async-start(), calls=%async_computation.13 | async-start | bytes 5242880 | tf_op jit(solution)/shard_map/while/body/eval_jaxpr/all_gather | solution.py:143
  16.5 120.7 %all-gather.13.cloned.1.call-start = ((), (), s32[]{:S(2)}) async-start(), calls=%async_computation.14 | async-start | bytes 1179648 | tf_op jit(solution)/shard_map/while/body/eval_jaxpr/all_gather | solution.py:137
  17.2 194.8 %all-gather.15.cloned.1.call-start = ((), (), s32[]{:S(2)}) async-start(), calls=%async_computation.15 | async-start | bytes 1179648 | tf_op jit(solution)/shard_map/while/body/eval_jaxpr/all_gather | solution.py:136
  17.8 213.9 %all-gather.17.cloned.1.call-start = ((), (), s32[]{:S(2)}) async-start(), calls=%async_computation.16 | async-start | bytes 5242880 | tf_op jit(solution)/shard_map/while/body/eval_jaxpr/all_gather | solution.py:188
  21.9 493.2 %all-gather.21.cloned.1.call-start = ((), (), s32[]{:S(2)}) async-start(), calls=%async_computation.18 | async-start | bytes 5242880 | tf_op jit(solution)/shard_map/while/body/eval_jaxpr/all_gather | solution.py:176
  44.4 203.2 %copy-start.56 = (f32[512]{0:T(512)}, f32[512]{0:T(512)S(1)}, u32[]{:S(2)}) copy-start(f32[512]{0:T(512)S(1)} %mul.1764) | copy-start | bytes 6148 | tf_op jit(solution)/shard_map/while
  104.0 437.8 %reduce-scatter.17.cloned.1.call-start = ((), (), s32[]{:S(2)}) async-start(), calls=%async_computation.19 | async-start | bytes 5242880 | tf_op jit(solution)/shard_map/while/body/eval_jaxpr/reduce_scatter | solution.py:240
  469.0 43.7 %all-to-all-start = ((bf16[4,512,512]{2,1,0:T(8,128)(2,1)}), bf16[4,512,512]{2,1,0:T(8,128)(2,1)S(1)}, u32[]{:S(2)}, u32[]{:S(2)}) async-start(bf16[4,512,512]{2,1,0:T(8,128)(2,1)} %pad_maximum_fusion.2), calls=%async_computation | async-start | bytes 4194304 | tf_op jit(solution)/shard_map/while/body/eval_jaxpr/all_to_all | solution.py:168
  521.5 17.9 %all-to-all-start.1 = ((bf16[512,4,256]{2,0,1:T(8,128)(2,1)}), bf16[512,4,256]{2,0,1:T(8,128)(2,1)S(1)}, u32[]{:S(2)}, u32[]{:S(2)}) async-start(bf16[512,4,256]{2,0,1:T(8,128)(2,1)} %bitcast.431), calls=%async_computation.1 | async-start | bytes 2097152 | tf_op jit(solution)/shard_map/while/body/eval_jaxpr/all_to_all | solution.py:177
  545.1 84.6 %all-gather.19.cloned.1.call-start = ((), (), s32[]{:S(2)}) async-start(), calls=%async_computation.17 | async-start | bytes 1179648 | tf_op jit(solution)/shard_map/while/body/eval_jaxpr/all_gather | solution.py:140
  545.9 83.9 %all-gather.11.cloned.1.call-start = ((), (), s32[]{:S(2)}) async-start(), calls=%async_computation.13 | async-start | bytes 5242880 | tf_op jit(solution)/shard_map/while/body/eval_jaxpr/all_gather | solution.py:143
  548.2 114.2 %all-gather.13.cloned.1.call-start = ((), (), s32[]{:S(2)}) async-start(), calls=%async_computation.14 | async-start | bytes 1179648 | tf_op jit(solution)/shard_map/while/body/eval_jaxpr/all_gather | solution.py:137
  548.8 188.1 %all-gather.15.cloned.1.call-start = ((), (), s32[]{:S(2)}) async-start(), calls=%async_computation.15 | async-start | bytes 1179648 | tf_op jit(solution)/shard_map/while/body/eval_jaxpr/all_gather | solution.py:136
  549.6 207.3 %all-gather.17.cloned.1.call-start = ((), (), s32[]{:S(2)}) async-start(), calls=%async_computation.16 | async-start | bytes 5242880 | tf_op jit(solution)/shard_map/while/body/eval_jaxpr/all_gather | solution.py:188
  553.7 486.8 %all-gather.21.cloned.1.call-start = ((), (), s32[]{:S(2)}) async-start(), calls=%async_computation.18 | async-start | bytes 5242880 | tf_op jit(solution)/shard_map/while/body/eval_jaxpr/all_gather | solution.py:176
  629.7 437.6 %reduce-scatter.17.cloned.1.call-start = ((), (), s32[]{:S(2)}) async-start(), calls=%async_computation.19 | async-start | bytes 5242880 | tf_op jit(solution)/shard_map/while/body/eval_jaxpr/reduce_scatter | solution.py:240
  994.1 44.0 %all-to-all-start = ((bf16[4,512,512]{2,1,0:T(8,128)(2,1)}), bf16[4,512,512]{2,1,0:T(8,128)(2,1)S(1)}, u32[]{:S(2)}, u32[]{:S(2)}) async-start(bf16[4,512,512]{2,1,0:T(8,128)(2,1)} %pad_maximum_fusion.2), calls=%async_computation | async-start | bytes 4194304 | tf_op jit(solution)/shard_map/while/body/eval_jaxpr/all_to_all | solution.py:168
  1046.8 18.1 %all-to-all-start.1 = ((bf16[512,4,256]{2,0,1:T(8,128)(2,1)}), bf16[512,4,256]{2,0,1:T(8,128)(2,1)S(1)}, u32[]{:S(2)}, u32[]{:S(2)}) async-start(bf16[512,4,256]{2,0,1:T(8,128)(2,1)} %bitcast.431), calls=%async_computation.1 | async-start | bytes 2097152 | tf_op jit(solution)/shard_map/while/body/eval_jaxpr/all_to_all | solution.py:177
  1072.5 78.3 %reduce-scatter.13.cloned.1.call-start = ((), (), s32[]{:S(2)}) async-start(), calls=%async_computation.11 | async-start | bytes 36864 | tf_op jit(solution)/shard_map/reduce_scatter | solution.py:298
  1073.1 192.8 %reduce-scatter.11.cloned.1.call-start = ((), (), s32[]{:S(2)}) async-start(), calls=%async_computation.10 | async-start | bytes 1081344 | tf_op jit(solution)/shard_map/reduce_scatter | solution.py:302
  1073.7 260.4 %reduce-scatter.7.cloned.1.call-start = ((), (), s32[]{:S(2)}) async-start(), calls=%async_computation.8 | async-start | bytes 2359296 | tf_op jit(solution)/shard_map/reduce_scatter | solution.py:296
  1074.2 331.5 %reduce-scatter.9.cloned.1.call-start = ((), (), s32[]{:S(2)}) async-start(), calls=%async_computation.9 | async-start | bytes 2359296 | tf_op jit(solution)/shard_map/reduce_scatter | solution.py:297
  1075.0 402.0 %reduce-scatter.15.cloned.1.call-start = ((), (), s32[]{:S(2)}) async-start(), calls=%async_computation.12 | async-start | bytes 2359296 | tf_op jit(solution)/shard_map/reduce_scatter | solution.py:299
  (191 other events, 2873.8 us)
Sparse Core Ops, SparseCore 0:
  16.3 42.9 all-gather.18
  60.9 33.7 all-gather.10
  96.8 40.3 all-gather.12
  139.2 38.9 all-gather.14
  179.6 33.7 all-gather.16
  214.8 34.9 all-gather.20
  465.8 56.6 reduce-scatter.16
  548.1 36.7 all-gather.18
  586.4 33.6 all-gather.10
  622.2 40.2 all-gather.12
  664.6 38.9 all-gather.14
  705.0 33.6 all-gather.16
  740.4 34.9 all-gather.20
  990.8 56.7 reduce-scatter.16
Sparse Core Ops, SparseCore 1:
  1076.7 51.0 reduce-scatter.12
  1130.4 135.4 reduce-scatter.10
  1269.9 64.2 reduce-scatter.6
  1338.2 67.4 reduce-scatter.8
  1409.9 67.1 reduce-scatter.14
